TPU v7x, 32 devices: a whole 2x2x4 slice. The times are simulated.
32 devices in a mesh: gx: 8 (over z, y), gy: 4 (over x, core).
Axes of the slice: x: 2, y: 2, z: 4, core: 2. Of those that a mesh axis runs over, the one named last changes fastest.
Arguments:
- fuel: float32 [16, 768, 384], P('gx', 'gy'), may hold values from -41 to 41, as said below
- oxidizer: float32 [16, 768, 384], P('gx', 'gy'), may hold values from -41 to 41, as said below
- kappa: float32 [16, 768, 384], P('gx', 'gy'), may hold values from 0.05 to 0.5
- rate: float32 [16, 768, 384], P('gx', 'gy'), may hold values from 0.5 to 5
Outputs:
- fuel_next: float32 [16, 768, 384], P('gx', 'gy')
- oxid_next: float32 [16, 768, 384], P('gx', 'gy')
- r_factor: float32 [384, 384], replicated
Inputs may be any that keep to these rules, and one draw needn't show every extreme that they name: `fuel`: A real-valued field. `oxidizer`: A real-valued field.
All inputs are finite; a program needn't handle non-finite values.
Results may differ from a plain program's by a relative error of at most 0.000067.
Values sent between devices are 32-bit elements; how exact they have to be, the bound alone decides.
A program may use at most 64 MiB of HBM per device.

v0:
```python
import jax
import jax.numpy as jnp
from jax import lax
from jax.sharding import PartitionSpec as P


def extended(cells, sides, width):
    for axis, dim in sides:
        count = lax.axis_size(axis)
        ends = count - 1
        head = lax.slice_in_dim(cells, 0, width, axis=dim)
        tail = lax.slice_in_dim(cells, cells.shape[dim] - width, cells.shape[dim], axis=dim)
        cells = jnp.concatenate(
            [
                lax.ppermute(tail, axis, [(i, (i + 1) % count) for i in range(ends)]),
                cells,
                lax.ppermute(head, axis, [((i + 1) % count, i) for i in range(ends)]),
            ],
            axis=dim,
        )
    return cells


def diffuse_local(padded, kpad):
    planes = padded.shape[0] - 2
    width = padded.shape[1] - 2
    total = jnp.zeros((planes, width, padded.shape[2] - 2), jnp.float32)
    center = padded[1:-1, 1:-1, 1:-1]
    kcenter = kpad[1:-1, 1:-1, 1:-1]
    sizes = (planes, width, padded.shape[2] - 2)
    for axis in range(3):
        for offset in (0, 2):
            index = [slice(1, -1)] * 3
            index[axis] = slice(offset, offset + sizes[axis])
            index = tuple(index)
            total = total + 0.5 * (kcenter + kpad[index]) * (padded[index] - center)
    return total


def local_gram(first, second):
    flat_a = first.reshape(-1, first.shape[2])
    flat_b = second.reshape(-1, second.shape[2])
    dims = (((0,), (0,)), ((), ()))
    gram = lax.dot_general(flat_a, flat_a, dims, precision=lax.Precision.HIGHEST)
    return gram + lax.dot_general(flat_b, flat_b, dims, precision=lax.Precision.HIGHEST)


def shards(fuel, oxidizer, kappa, rate):
    stacked = jnp.stack([fuel, oxidizer, kappa])
    widened = extended(stacked, (("gx", 1), ("gy", 2)), 1)
    widened = jnp.pad(widened, ((0, 0), (0, 0), (0, 0), (1, 1)))
    prod = fuel * oxidizer
    react = rate * prod / jnp.sqrt(1.0 + prod * prod)
    fuel_next = fuel + 0.15 * (diffuse_local(widened[0], widened[2]) - react)
    oxid_next = oxidizer + 0.15 * (diffuse_local(widened[1], widened[2]) + react)
    rows = 2 * fuel.shape[0] * fuel.shape[1] * lax.axis_size("gx") * lax.axis_size("gy")
    gram = local_gram(fuel_next, oxid_next) / rows
    total = lax.psum(gram, ("gx", "gy"))
    factor = jnp.linalg.cholesky(total).T
    return (fuel_next, oxid_next, factor)


def solution(mesh):
    in_specs = (P("gx", "gy", None), P("gx", "gy", None), P("gx", "gy", None), P("gx", "gy", None))
    out_specs = (P("gx", "gy", None), P("gx", "gy", None), P())
    return jax.shard_map(shards, mesh=mesh, in_specs=in_specs, out_specs=out_specs, check_vma=False)
```

profile of v0, /device:TPU:0, one launch (start us, length us, event | category | flops | bytes accessed | tf_op | source)
XLA Modules:
  0.0 272.9 jit_solution(1757577690455986732)
XLA Ops:
  7.2 1.7 pad_maximum_fusion
  9.0 5.0 %collective-permute-start = (f32[3,1,192,384]{3,2,1,0:T(8,128)S(1)}, f32[3,1,192,384]{3,2,1,0:T(8,128)S(1)}, u32[]{:S(2)}, u32[]{:S(2)}) collective-permute-start(f32[3,1,192,384]{3,2,1,0:T(8,128)S(1)} %get-tuple-element.11), channel_id=1, source_target_pairs={{0,4},{4,8},{8,12},{12,16},{16,20},{20,24},{24,28},{1,5},{5,9},{9,... | collective-permute-start | bytes 2654216 | tf_op jit(solution)/shard_map/ppermute | solution.py:15
  14.0 1.3 collective-permute-start.1
  15.3 36.5 %collective-permute-done = f32[3,1,192,384]{3,2,1,0:T(8,128)S(1)} collective-permute-done((f32[3,1,192,384]{3,2,1,0:T(8,128)S(1)}, f32[3,1,192,384]{3,2,1,0:T(8,128)S(1)}, u32[]{:S(2)}, u32[]{:S(2)}) %collective-permute-start) | collective-permute-done | bytes 884768 | tf_op jit(solution)/shard_map/ppermute | solution.py:15
  51.8 1.3 collective-permute-start.2
  53.1 1.3 collective-permute-start.3
  54.4 3.5 %collective-permute-done.3 = f32[3,4,1,384]{3,2,1,0:T(1,128)S(1)} collective-permute-done((f32[3,4,1,384]{3,2,1,0:T(1,128)S(1)}, f32[3,4,1,384]{3,2,1,0:T(1,128)S(1)}, u32[]{:S(2)}, u32[]{:S(2)}) %collective-permute-start.3) | collective-permute-done | bytes 18464 | tf_op jit(solution)/shard_map/ppermute | solution.py:17
  57.9 4.8 %select_maximum_fusion = f32[3,4,194,386]{3,2,1,0:T(8,128)S(1)} fusion(f32[3,4,1,384]{3,2,1,0:T(1,128)S(1)} %collective-permute-done.3, f32[3,4,1,384]{3,2,1,0:T(1,128)S(1)} %collective-permute-done.2, f32[3,1,192,384]{3,2,1,0:T(8,128)S(1)} %collective-permute-done.1, f32[3,1,192,384]{3,2,1,0:T(8,128)S(1)} %collective-permute-done, ...), kind=kLoop, calls=%fused_computation.2 | loop fusion | flops 14377728 | bytes 7170240 | tf_op jit(solution)/shard_map/concatenate | solution.py:13
  62.7 0.5 slice_bitcast_fusion
  63.8 2.0 fusion.7
  65.8 2.0 fusion.21
  67.9 1.4 convolution_bitcast_fusion
  69.3 2.2 fusion.2
  71.5 131.7 %all-reduce.4.cloned.1.call-done = f32[384,384]{0,1:T(8,128)} async-done(((f32[384,384]{0,1:T(8,128)}), f32[384,384]{0,1:T(8,128)}) %all-reduce.4.cloned.1.call-update) | async-done | bytes 589840 | tf_op jit(solution)/shard_map/psum | solution.py:58
  203.2 1.3 copy.9
  204.5 1.1 fusion.37
  205.6 11.7 %cholesky.77 = f32[128,128]{1,0:T(8,128)S(1)} custom-call(f32[128,128]{1,0:T(8,128)S(1)} %cholesky.192), custom_call_target="Cholesky" | custom-call | tf_op jit(solution)/shard_map/jit(cholesky)/cholesky | solution.py:59
  217.4 10.0 %custom-call.19 = f32[1,128,128]{1,2,0:T(8,128)S(1)} custom-call(f32[1,128,128]{2,1,0:T(8,128)S(1)} %get-tuple-element.19), custom_call_target="InvertDiagBlocksLowerTriangular" | custom-call | tf_op jit(solution)/shard_map/jit(cholesky)/cholesky | solution.py:59
  228.0 11.7 %cholesky.162 = f32[128,128]{1,0:T(8,128)S(1)} custom-call(f32[128,128]{1,0:T(8,128)S(1)} %cholesky.196), custom_call_target="Cholesky" | custom-call | tf_op jit(solution)/shard_map/jit(cholesky)/cholesky | solution.py:59
  239.7 9.8 %custom-call.20 = f32[1,128,128]{1,2,0:T(8,128)S(1)} custom-call(f32[1,128,128]{2,1,0:T(8,128)S(1)} %get-tuple-element.16), custom_call_target="InvertDiagBlocksLowerTriangular" | custom-call | tf_op jit(solution)/shard_map/jit(cholesky)/cholesky | solution.py:59
  250.0 11.7 %cholesky.181 = f32[128,128]{1,0:T(8,128)S(1)} custom-call(f32[128,128]{1,0:T(8,128)S(1)} %convolution_subtract_fusion.1), custom_call_target="Cholesky" | custom-call | tf_op jit(solution)/shard_map/jit(cholesky)/cholesky | solution.py:59
  261.8 0.6 compare_reduce_fusion
  262.4 0.7 compare_reduce_fusion.1
  265.0 1.1 copy.10
  (29 shorter events, 2.0 us)
Async XLA Ops:
  7.2 44.6 %copy-start.1 = (f32[2,192,384]{2,1,0:T(8,128)S(1)}, f32[2,192,384]{2,1,0:T(8,128)}, u32[]{:S(2)}) copy-start(f32[2,192,384]{2,1,0:T(8,128)} %param.5) | copy-start | bytes 1769476
  7.2 44.6 %copy-start = (f32[2,192,384]{2,1,0:T(8,128)S(1)}, f32[2,192,384]{2,1,0:T(8,128)}, u32[]{:S(2)}) copy-start(f32[2,192,384]{2,1,0:T(8,128)} %param.4) | copy-start | bytes 1769476
  7.2 44.6 %copy-start.2 = (f32[2,192,384]{2,1,0:T(8,128)S(1)}, f32[2,192,384]{2,1,0:T(8,128)}, u32[]{:S(2)}) copy-start(f32[2,192,384]{2,1,0:T(8,128)} %param.6) | copy-start | bytes 1769476
  7.2 196.0 %all-reduce.4.cloned.1.call-start = ((), (), s32[]{:S(2)}) async-start(), calls=%async_computation | async-start | bytes 1179648 | tf_op jit(solution)/shard_map/psum | solution.py:58
  9.0 42.8 %collective-permute-start = (f32[3,1,192,384]{3,2,1,0:T(8,128)S(1)}, f32[3,1,192,384]{3,2,1,0:T(8,128)S(1)}, u32[]{:S(2)}, u32[]{:S(2)}) collective-permute-start(f32[3,1,192,384]{3,2,1,0:T(8,128)S(1)} %get-tuple-element.11), channel_id=1, source_target_pairs={{0,4},{4,8},{8,12},{12,16},{16,20},{20,24},{24,28},{1,5},{5,9},{9,... | collective-permute-start | bytes 2654216 | tf_op jit(solution)/shard_map/ppermute | solution.py:15
  14.0 37.8 %collective-permute-start.1 = (f32[3,1,192,384]{3,2,1,0:T(8,128)S(1)}, f32[3,1,192,384]{3,2,1,0:T(8,128)S(1)}, u32[]{:S(2)}, u32[]{:S(2)}) collective-permute-start(f32[3,1,192,384]{3,2,1,0:T(8,128)S(1)} %get-tuple-element.12), channel_id=1, source_target_pairs={{4,0},{8,4},{12,8},{16,12},{20,16},{24,20},{28,24},{5,1},{9,5},{13... | collective-permute-start | bytes 2654216 | tf_op jit(solution)/shard_map/ppermute | solution.py:17
  51.8 2.6 collective-permute-start.2
  53.1 4.8 %collective-permute-start.3 = (f32[3,4,1,384]{3,2,1,0:T(1,128)S(1)}, f32[3,4,1,384]{3,2,1,0:T(1,128)S(1)}, u32[]{:S(2)}, u32[]{:S(2)}) collective-permute-start(f32[3,4,1,384]{3,2,1,0:T(1,128)S(1)} %get-tuple-element.10), channel_id=1, source_target_pairs={{1,0},{2,1},{3,2},{5,4},{6,5},{7,6},{9,8},{10,9},{11,10},{13,12},{... | collective-permute-start | bytes 55304 | tf_op jit(solution)/shard_map/ppermute | solution.py:17
  62.7 1.1 copy-start.5
  65.8 2.1 copy-start.3
  67.9 171.8 %copy-start.4 = (f32[2,192,384]{2,1,0:T(8,128)}, f32[2,192,384]{2,1,0:T(8,128)S(1)}, u32[]{:S(2)}) copy-start(f32[2,192,384]{2,1,0:T(8,128)S(1)} %fusion.21) | copy-start | bytes 1769476
Sparse Core Ops, SparseCore 0:
  71.6 131.5 all-reduce.3
where the time goes:
time: 273 us
  waiting for transfers between devices  172 us (63%)
  other arithmetic  68 us (25%)
  between operations  16.1 us (6%)
  starting transfers between devices  8.87 us (3%)
  matrix products  4.56 us (2%)
  local copies, waits for them, and re-layouts  3.59 us (1%)
    psum x1, waiting for transfers between devices, shards(): total = lax.psum(gram, ('gx', 'gy'))  132 us
    another operation x10, other arithmetic, shards(): factor = jnp.linalg.cholesky(total).T  56.3 us
    ppermute x2, waiting for transfers between devices, extended(): lax.ppermute(tail, axis, [(i, (i + 1) % count) for i in range(ends)])  36.5 us
    ppermute x2, starting transfers between devices, extended(): lax.ppermute(tail, axis, [(i, (i + 1) % count) for i in range(ends)])  6.25 us
  transfers between devices with their start and end apart: 5, of which 3 were waited for; matrix products, arithmetic and copies ran while one was open for 0% of the time, Pallas kernels for 0%

commit v1 on v0

v1 whole, which is shorter than its diff:
```python
import functools

import jax
import jax.numpy as jnp
from jax import lax
from jax.experimental import pallas as pl
from jax.experimental.pallas import tpu as pltpu
from jax.sharding import PartitionSpec as P

MESH = pl.DeviceIdType.MESH
TILE = 8
LANES = 128
HIGHEST = lax.Precision.HIGHEST


def halo_kernel(n, m, f_ref, o_ref, k_ref, xlo, xhi, ylo, yhi, send_sem, recv_sem):
    i, j = lax.axis_index("gx"), lax.axis_index("gy")
    planes, width = f_ref.shape[0], f_ref.shape[1]
    sides = (
        (i < n - 1, i > 0, i + 1, j),
        (i > 0, i < n - 1, i - 1, j),
        (j < m - 1, j > 0, i, j + 1),
        (j > 0, j < m - 1, i, j - 1),
    )
    barrier = pltpu.get_barrier_semaphore()
    for has, _, a, b in sides:
        @pl.when(has)
        def _(a=a, b=b):
            pl.semaphore_signal(barrier, inc=1, device_id=(a, b), device_id_type=MESH)
    pl.semaphore_wait(barrier, sum(has.astype(jnp.int32) for has, _, _, _ in sides))
    outs = (xlo, xhi, ylo, yhi)

    def copies(side, a, b):
        made = []
        for t, ref in enumerate((f_ref, o_ref, k_ref)):
            src = (
                ref.at[planes - 1],
                ref.at[0],
                ref.at[:, pl.ds(width - TILE, TILE)],
                ref.at[:, pl.ds(0, TILE)],
            )[side]
            made.append(
                pltpu.make_async_remote_copy(
                    src_ref=src,
                    dst_ref=outs[side].at[t],
                    send_sem=send_sem.at[side, t],
                    recv_sem=recv_sem.at[side, t],
                    device_id=(a, b),
                    device_id_type=MESH,
                )
            )
        return made

    for side, (has, _, a, b) in enumerate(sides):
        @pl.when(has)
        def _(side=side, a=a, b=b):
            for copy in copies(side, a, b):
                copy.start()
    for side, (has, gets, a, b) in enumerate(sides):
        @pl.when(has)
        def _(side=side, a=a, b=b):
            for copy in copies(side, a, b):
                copy.wait_send()

        @pl.when(gets)
        def _(side=side, a=a, b=b):
            for copy in copies(side, a, b):
                copy.wait_recv()


def halo(n, m, fuel, oxidizer, kappa):
    planes, width, depth = fuel.shape
    any_spec = pl.BlockSpec(memory_space=pl.ANY)
    xs = jax.ShapeDtypeStruct((3, width, depth), jnp.float32)
    ys = jax.ShapeDtypeStruct((3, planes, TILE, depth), jnp.float32)
    return pl.pallas_call(
        functools.partial(halo_kernel, n, m),
        out_shape=(xs, xs, ys, ys),
        in_specs=[any_spec] * 3,
        out_specs=(any_spec,) * 4,
        scratch_shapes=[pltpu.SemaphoreType.DMA((4, 3)), pltpu.SemaphoreType.DMA((4, 3))],
        compiler_params=pltpu.CompilerParams(collective_id=0, has_side_effects=True),
        name="halo",
    )(fuel, oxidizer, kappa)


def stencil_kernel(n, m, rows, step, f_ref, o_ref, k_ref, r_ref, xlo, xhi, ylo, yhi, fn_ref, on_ref, g_ref):
    i, j = lax.axis_index("gx"), lax.axis_index("gy")
    planes, width, depth = f_ref.shape
    row = lax.broadcasted_iota(jnp.int32, (step, depth), 0)
    lane = lax.broadcasted_iota(jnp.int32, (step, depth), 1)
    refs = (f_ref, o_ref, k_ref)
    zero = jnp.zeros((step, depth), jnp.float32)
    zrow = jnp.zeros((1, depth), jnp.float32)
    for x in range(planes):
        for y in range(0, width, step):
            part = pl.ds(y, step)
            center = [ref[x, part] for ref in refs]
            sets = []
            if x == 0:
                sets.append([jnp.where(i > 0, xlo[t, part], zero) for t in range(3)])
            else:
                sets.append([ref[x - 1, part] for ref in refs])
            if x == planes - 1:
                sets.append([jnp.where(i < n - 1, xhi[t, part], zero) for t in range(3)])
            else:
                sets.append([ref[x + 1, part] for ref in refs])
            if y == 0:
                before = [jnp.where(j > 0, ylo[t, x, TILE - 1:TILE], zrow) for t in range(3)]
            else:
                before = [ref[x, y - 1:y] for ref in refs]
            if y + step == width:
                after = [jnp.where(j < m - 1, yhi[t, x, 0:1], zrow) for t in range(3)]
            else:
                after = [ref[x, y + step:y + step + 1] for ref in refs]
            sets.append([jnp.where(row == 0, b, pltpu.roll(c, 1, 0)) for b, c in zip(before, center)])
            sets.append([jnp.where(row == step - 1, a, pltpu.roll(c, step - 1, 0)) for a, c in zip(after, center)])
            sets.append([jnp.where(lane == 0, 0.0, pltpu.roll(c, 1, 1)) for c in center])
            sets.append([jnp.where(lane == depth - 1, 0.0, pltpu.roll(c, depth - 1, 1)) for c in center])
            fc, oc, kc = center
            df, do = zero, zero
            for fs, os, ks in sets:
                weight = 0.5 * (kc + ks)
                df = df + weight * (fs - fc)
                do = do + weight * (os - oc)
            prod = fc * oc
            react = r_ref[x, part] * prod / jnp.sqrt(1.0 + prod * prod)
            fn_ref[x, part] = fc + 0.15 * (df - react)
            on_ref[x, part] = oc + 0.15 * (do + react)
    dims = (((0,), (0,)), ((), ()))
    at = 0
    flat = [ref[...].reshape(planes * width, depth) for ref in (fn_ref, on_ref)]
    for a in range(0, depth, LANES):
        total = sum(
            lax.dot_general(u[:, a:a + LANES], u[:, a:], dims, precision=HIGHEST, preferred_element_type=jnp.float32)
            for u in flat
        ) / rows
        for b in range(0, depth - a, LANES):
            g_ref[at:at + LANES] = total[:, b:b + LANES]
            at += LANES


def stencil(n, m, rows, fuel, oxidizer, kappa, rate, halos):
    planes, width, depth = fuel.shape
    blocks = depth // LANES
    field = jax.ShapeDtypeStruct(fuel.shape, jnp.float32)
    vmem = pl.BlockSpec(memory_space=pltpu.VMEM)
    return pl.pallas_call(
        functools.partial(stencil_kernel, n, m, rows, 32),
        out_shape=(field, field, jax.ShapeDtypeStruct((blocks * (blocks + 1) // 2 * LANES, LANES), jnp.float32)),
        in_specs=[vmem] * 8,
        out_specs=(vmem,) * 3,
        name="stencil",
    )(fuel, oxidizer, kappa, rate, *halos)


def sum_kernel(stages, g_ref, out_ref, *scratch):
    count = len(stages)
    inbox, held, sems = scratch[:count], scratch[count:2 * count], scratch[2 * count:]
    index = {"gx": lax.axis_index("gx"), "gy": lax.axis_index("gy")}

    def peer(stage, k):
        axis, stride, size = stage
        mine = lax.rem(index[axis] // stride, size)
        other = lax.rem(mine + k, size)
        place = dict(index)
        place[axis] = index[axis] + (other - mine) * stride
        return mine, other, (place["gx"], place["gy"])

    barrier = pltpu.get_barrier_semaphore()
    greeted = 0
    for stage in stages:
        for k in range(1, stage[2]):
            pl.semaphore_signal(barrier, inc=1, device_id=peer(stage, k)[2], device_id_type=MESH)
            greeted += 1
    pl.semaphore_wait(barrier, greeted)
    source = g_ref
    length = g_ref.shape[0]
    starts = []
    start = 0
    for s, stage in enumerate(stages):
        size = stage[2]
        length //= size
        sent = []
        for k in range(1, size):
            mine, other, device = peer(stage, k)
            sent.append(
                pltpu.make_async_remote_copy(
                    src_ref=source.at[pl.ds(pl.multiple_of(other * length, TILE), length)],
                    dst_ref=inbox[s].at[k - 1],
                    send_sem=sems[0].at[s, k - 1],
                    recv_sem=sems[1].at[s, k - 1],
                    device_id=device,
                    device_id_type=MESH,
                )
            )
            sent[-1].start()
        for copy in sent:
            copy.wait_recv()
        total = source[pl.ds(pl.multiple_of(mine * length, TILE), length)]
        for k in range(1, size):
            total = total + inbox[s][k - 1]
        held[s][...] = total
        for copy in sent:
            copy.wait_send()
        source = held[s]
        start = start + mine * length
        starts.append((start, length))
    part = pl.ds(pl.multiple_of(start, TILE), length)
    out_ref[part] = source[...]
    for s in reversed(range(count)):
        stage = stages[s]
        start, length = starts[s]
        part = pl.ds(pl.multiple_of(start, TILE), length)
        sent = []
        for k in range(1, stage[2]):
            sent.append(
                pltpu.make_async_remote_copy(
                    src_ref=out_ref.at[part],
                    dst_ref=out_ref.at[part],
                    send_sem=sems[2].at[s, k - 1],
                    recv_sem=sems[3].at[s, k - 1],
                    device_id=peer(stage, k)[2],
                    device_id_type=MESH,
                )
            )
            sent[-1].start()
        for copy in sent:
            copy.wait()


def sum_over_all(stages, gram):
    length, lanes = gram.shape
    inbox, held = [], []
    most = max(stage[2] for stage in stages)
    for _, _, size in stages:
        length //= size
        inbox.append(pltpu.VMEM((size - 1, length, lanes), jnp.float32))
        held.append(pltpu.VMEM((length, lanes), jnp.float32))
    vmem = pl.BlockSpec(memory_space=pltpu.VMEM)
    return pl.pallas_call(
        functools.partial(sum_kernel, stages),
        out_shape=jax.ShapeDtypeStruct(gram.shape, jnp.float32),
        in_specs=[vmem],
        out_specs=vmem,
        scratch_shapes=[*inbox, *held] + [pltpu.SemaphoreType.DMA((len(stages), most - 1))] * 4,
        compiler_params=pltpu.CompilerParams(collective_id=1, has_side_effects=True),
        name="allsum",
    )(gram)


def factor_kernel(g_ref, r_ref, a_ref):
    depth = r_ref.shape[0]
    blocks = depth // LANES
    at = 0
    for b in range(blocks):
        for c in range(b, blocks):
            a_ref[b * LANES:(b + 1) * LANES, c * LANES:(c + 1) * LANES] = g_ref[at:at + LANES]
            at += LANES
    dims = (((0,), (0,)), ((), ()))
    dot = functools.partial(lax.dot_general, dimension_numbers=dims, precision=HIGHEST, preferred_element_type=jnp.float32)
    for b in range(blocks):
        c0 = b * LANES
        wide = depth - c0
        sub = lax.broadcasted_iota(jnp.int32, (TILE, wide), 0)
        lane = lax.broadcasted_iota(jnp.int32, (TILE, wide), 1)
        if c0:
            r_ref[c0:c0 + LANES, :c0] = jnp.zeros((LANES, c0), jnp.float32)
        for p in range(0, LANES, TILE):
            r0 = c0 + p
            panel = a_ref[r0:r0 + TILE, c0:]
            e = {}
            for k in range(TILE):
                column = jnp.broadcast_to(panel[:, p + k:p + k + 1], (TILE, LANES))
                for i in range(k, TILE):
                    e[i, k] = jnp.broadcast_to(column[i:i + 1], (TILE, LANES))
            inv, low = [], {}
            for k in range(TILE):
                inv.append(lax.rsqrt(e[k, k]))
                for i in range(k + 1, TILE):
                    low[i, k] = e[i, k] * inv[k]
                for j in range(k + 1, TILE):
                    for i in range(j, TILE):
                        e[i, j] = e[i, j] - low[i, k] * low[j, k]
            done = [[] for _ in range(TILE)]
            strips = []
            for c in range(0, wide, LANES):
                rows = []
                for k in range(TILE):
                    value = jnp.broadcast_to(panel[k:k + 1, c:c + LANES], (TILE, LANES))
                    for j in range(k):
                        value = value - low[k, j] * rows[j]
                    rows.append(value * inv[k])
                strip = rows[0]
                for k in range(1, TILE):
                    strip = jnp.where(sub[:, :LANES] == k, rows[k], strip)
                strips.append(strip)
            strips[0] = jnp.where(lane[:, :LANES] >= sub[:, :LANES] + p, strips[0], 0.0)
            upper = strips[0] if len(strips) == 1 else jnp.concatenate(strips, axis=1)
            r_ref[r0:r0 + TILE, c0:] = upper
            if p + TILE < LANES:
                change = dot(upper[:, :LANES], upper)
                a_ref[r0 + TILE:c0 + LANES, c0:] -= change[p + TILE:]
        for d in range(b + 1, blocks):
            d0 = d * LANES
            a_ref[d0:d0 + LANES, d0:] -= dot(r_ref[c0:c0 + LANES, d0:d0 + LANES], r_ref[c0:c0 + LANES, d0:])


def factor(gram, depth):
    vmem = pl.BlockSpec(memory_space=pltpu.VMEM)
    return pl.pallas_call(
        factor_kernel,
        out_shape=jax.ShapeDtypeStruct((depth, depth), jnp.float32),
        in_specs=[vmem],
        out_specs=vmem,
        scratch_shapes=[pltpu.VMEM((depth, depth), jnp.float32)],
        name="factor",
    )(gram)


def shards(n, m, fuel, oxidizer, kappa, rate):
    planes, width, depth = fuel.shape
    rows = 2 * planes * width * n * m
    halos = halo(n, m, fuel, oxidizer, kappa)
    fuel_next, oxid_next, gram = stencil(n, m, rows, fuel, oxidizer, kappa, rate, halos)
    pairs = [("gy", 1, 2), ("gy", 2, 2)] if m == 4 else [("gy", 1, m)]
    stages = tuple(pairs + [("gx", 1, n)])
    if gram.shape[0] % (TILE * n * m) == 0:
        gram = sum_over_all(stages, gram)
    else:
        gram = lax.psum(gram, ("gx", "gy"))
    return (fuel_next, oxid_next, factor(gram, depth))


def solution(mesh):
    spec = P("gx", "gy", None)
    body = functools.partial(shards, mesh.shape["gx"], mesh.shape["gy"])
    return jax.shard_map(body, mesh=mesh, in_specs=(spec,) * 4, out_specs=(spec, spec, P()), check_vma=False)
```

time: 273 us -> 104 us (0.38)
  waiting for transfers between devices: 172 us -> 0 us
  Pallas kernels: 0 us -> 103 us
  other arithmetic: 68 us -> 0 us
  between operations: 16.1 us -> 0.65 us
  starting transfers between devices: 8.87 us -> 0 us
  matrix products: 4.56 us -> 0 us
  local copies, waits for them, and re-layouts: 3.59 us -> 0 us
    psum x1 -> x0, waiting for transfers between devices: 132 us -> none  [shards(): total = lax.psum(gram, ('gx', 'gy'))]
    pallas_call x0 -> x4, Pallas kernels: none -> 103 us  [the longest x1 42 us: halo(): pl.pallas_call(functools.partial(halo_kernel, n, m), out_shape=(xs, xs, y...]
    another operation x11 -> x0, other arithmetic: 58 us -> none  [the longest x10 56.3 us: shards(): factor = jnp.linalg.cholesky(total).T]
    ppermute x4 -> x0, waiting for transfers between devices: 40 us -> none  [the longest x2 36.5 us: extended(): lax.ppermute(tail, axis, [(i, (i + 1) % count) for i in range(ends)])]
    ppermute x4 -> x0, starting transfers between devices: 8.83 us -> none  [the longest x2 6.25 us: extended(): lax.ppermute(tail, axis, [(i, (i + 1) % count) for i in range(ends)])]
    concatenate x1 -> x0, other arithmetic: 4.77 us -> none  [extended(): jnp.concatenate([lax.ppermute(tail, axis, [(i, (i + 1) % count) for i in...]
    add x2 -> x0, other arithmetic: 4.08 us -> none  [the longest x1 2.04 us: shards(): fuel_next = fuel + 0.15 * (diffuse_local(widened[0], widened[2]) - react)]
    dot_general x2 -> x0, matrix products: 3.54 us -> none  [the longest x1 2.15 us: local_gram(): lax.dot_general(flat_a, flat_a, dims, precision=lax.Precision.HIGHEST)]
  transfers between devices with their start and end apart: 5 -> 0, of which waited for: 3 -> 0; matrix products, arithmetic and copies ran while one was open for 0% -> 0% of each run, Pallas kernels for 0% -> 0%
where the time goes in v1:
time: 104 us
  Pallas kernels  103 us (99%)
    pallas_call x1, Pallas kernels, halo(): pl.pallas_call(functools.partial(halo_kernel, n, m), out_shape=(xs, xs, y...  42 us
    pallas_call x1, Pallas kernels, factor(): pl.pallas_call(factor_kernel, out_shape=jax.ShapeDtypeStruct((depth, dept...  28.2 us
    pallas_call x1, Pallas kernels, sum_over_all(): pl.pallas_call(functools.partial(sum_kernel, stages), out_shape=jax.Shape...  26.1 us
    pallas_call x1, Pallas kernels, stencil(): pl.pallas_call(functools.partial(stencil_kernel, n, m, rows, 32), out_sha...  6.53 us

profile of v1, /device:TPU:0, one launch (start us, length us, event | category | flops | bytes accessed | tf_op | source)
XLA Modules:
  0.0 103.5 jit_solution(9255593457955545930)
XLA Ops:
  0.6 42.0 %halo.1 = (f32[3,192,384]{2,1,0:T(8,128)}, f32[3,192,384]{2,1,0:T(8,128)}, f32[3,2,8,384]{3,2,1,0:T(8,128)}, f32[3,2,8,384]{3,2,1,0:T(8,128)}) custom-call(f32[2,192,384]{2,1,0:T(8,128)} %f_ref.3, f32[2,192,384]{2,1,0:T(8,128)} %o_ref.3, f32[2,192,384]{2,1,0:T(8,128)} %k_ref.3), custom_call_target="tpu_custom_call" | custom-call | tf_op jit(solution)/shard_map/halo/pallas_call | solution.py:76
  42.6 6.5 %stencil.1 = (f32[2,192,384]{2,1,0:T(8,128)}, f32[2,192,384]{2,1,0:T(8,128)}, f32[768,128]{1,0:T(8,128)}) custom-call(f32[2,192,384]{2,1,0:T(8,128)} %f_ref.3, f32[2,192,384]{2,1,0:T(8,128)} %o_ref.3, f32[2,192,384]{2,1,0:T(8,128)} %k_ref.3, f32[2,192,384]{2,1,0:T(8,128)} %r_ref.1, f32[3,192,384]{2,1,0:T(8,128)} %get-tuple-element.10.xlo, ...), custom_call_target="tpu_custom_call" | custom-call | tf_op jit(solution)/shard_map/stencil/pallas_call | solution.py:148
  49.1 26.1 %allsum.1.g_ref = f32[768,128]{1,0:T(8,128)} custom-call(f32[768,128]{1,0:T(8,128)} %get-tuple-element.16.g_ref), custom_call_target="tpu_custom_call" | custom-call | tf_op jit(solution)/shard_map/allsum/pallas_call | solution.py:241
  75.3 28.2 %factor.1 = f32[384,384]{1,0:T(8,128)} custom-call(f32[768,128]{1,0:T(8,128)} %allsum.1.g_ref), custom_call_target="tpu_custom_call" | custom-call | tf_op jit(solution)/shard_map/factor/pallas_call | solution.py:311

commit v2 on v1

--- a/solution.py
+++ b/solution.py
@@ -249,7 +249,23 @@
     )(gram)
 
 
-def factor_kernel(g_ref, r_ref, a_ref):
+def stacked_dot(left, right):
+    dims = (((0,), (0,)), ((), ()))
+    def pieces(v):
+        h = v.astype(jnp.bfloat16).astype(jnp.float32)
+        m = (v - h).astype(jnp.bfloat16).astype(jnp.float32)
+        return h, m, v - h - m
+    (a, b, c), (d, e, f) = pieces(left), pieces(right)
+    lhs = jnp.concatenate([a, a, b, a, c, b], axis=0).astype(jnp.bfloat16)
+    rhs = jnp.concatenate([d, e, d, f, d, e], axis=0).astype(jnp.bfloat16)
+    return lax.dot_general(lhs, rhs, dims, preferred_element_type=jnp.float32)
+
+
+def column_of(panel, at):
+    return jnp.broadcast_to(panel[:, at:at + 1], (TILE, LANES))
+
+
+def factor_kernel(group, g_ref, r_ref, a_ref):
     depth = r_ref.shape[0]
     blocks = depth // LANES
     at = 0
@@ -259,48 +275,61 @@
             at += LANES
     dims = (((0,), (0,)), ((), ()))
     dot = functools.partial(lax.dot_general, dimension_numbers=dims, precision=HIGHEST, preferred_element_type=jnp.float32)
+    sub = lax.broadcasted_iota(jnp.int32, (TILE, LANES), 0)
+    lane = lax.broadcasted_iota(jnp.int32, (TILE, LANES), 1)
     for b in range(blocks):
         c0 = b * LANES
-        wide = depth - c0
-        sub = lax.broadcasted_iota(jnp.int32, (TILE, wide), 0)
-        lane = lax.broadcasted_iota(jnp.int32, (TILE, wide), 1)
+        tiles = range(blocks - b)
         if c0:
             r_ref[c0:c0 + LANES, :c0] = jnp.zeros((LANES, c0), jnp.float32)
-        for p in range(0, LANES, TILE):
-            r0 = c0 + p
-            panel = a_ref[r0:r0 + TILE, c0:]
-            e = {}
-            for k in range(TILE):
-                column = jnp.broadcast_to(panel[:, p + k:p + k + 1], (TILE, LANES))
-                for i in range(k, TILE):
-                    e[i, k] = jnp.broadcast_to(column[i:i + 1], (TILE, LANES))
-            inv, low = [], {}
-            for k in range(TILE):
-                inv.append(lax.rsqrt(e[k, k]))
-                for i in range(k + 1, TILE):
-                    low[i, k] = e[i, k] * inv[k]
-                for j in range(k + 1, TILE):
-                    for i in range(j, TILE):
-                        e[i, j] = e[i, j] - low[i, k] * low[j, k]
-            done = [[] for _ in range(TILE)]
-            strips = []
-            for c in range(0, wide, LANES):
+        for p in range(0, LANES, TILE * group):
+            before = []
+            for q in range(p, p + TILE * group, TILE):
+                r0 = c0 + q
+                strips = [a_ref[r0:r0 + TILE, c0 + t * LANES:c0 + (t + 1) * LANES] for t in tiles]
+                for s, inv, low, rows in before:
+                    factors = []
+                    for k in range(TILE):
+                        value = column_of(strips[0], s + k)
+                        for j in range(k):
+                            value = value - factors[j] * low[k, j]
+                        factors.append(value * inv[k])
+                    for t in tiles:
+                        for k in range(TILE):
+                            strips[t] = strips[t] - factors[k] * rows[t][k]
+                e = {}
+                for k in range(TILE):
+                    column = column_of(strips[0], q + k)
+                    for i in range(k, TILE):
+                        e[i, k] = jnp.broadcast_to(column[i:i + 1], (TILE, LANES))
+                inv, low = [], {}
+                for k in range(TILE):
+                    inv.append(lax.rsqrt(e[k, k]))
+                    for i in range(k + 1, TILE):
+                        low[i, k] = e[i, k] * inv[k]
+                    for j in range(k + 1, TILE):
+                        for i in range(j, TILE):
+                            e[i, j] = e[i, j] - low[i, k] * low[j, k]
                 rows = []
-                for k in range(TILE):
-                    value = jnp.broadcast_to(panel[k:k + 1, c:c + LANES], (TILE, LANES))
-                    for j in range(k):
-                        value = value - low[k, j] * rows[j]
-                    rows.append(value * inv[k])
-                strip = rows[0]
-                for k in range(1, TILE):
-                    strip = jnp.where(sub[:, :LANES] == k, rows[k], strip)
-                strips.append(strip)
-            strips[0] = jnp.where(lane[:, :LANES] >= sub[:, :LANES] + p, strips[0], 0.0)
-            upper = strips[0] if len(strips) == 1 else jnp.concatenate(strips, axis=1)
-            r_ref[r0:r0 + TILE, c0:] = upper
-            if p + TILE < LANES:
-                change = dot(upper[:, :LANES], upper)
-                a_ref[r0 + TILE:c0 + LANES, c0:] -= change[p + TILE:]
+                for t in tiles:
+                    made = []
+                    for k in range(TILE):
+                        value = jnp.broadcast_to(strips[t][k:k + 1], (TILE, LANES))
+                        for j in range(k):
+                            value = value - low[k, j] * made[j]
+                        made.append(value * inv[k])
+                    rows.append(made)
+                    strip = made[0]
+                    for k in range(1, TILE):
+                        strip = jnp.where(sub == k, made[k], strip)
+                    if t == 0:
+                        strip = jnp.where(lane >= sub + q, strip, 0.0)
+                    r_ref[r0:r0 + TILE, c0 + t * LANES:c0 + (t + 1) * LANES] = strip
+                before.append((q, inv, low, rows))
+            low_end = p + TILE * group
+            if low_end < LANES:
+                upper = r_ref[c0 + p:c0 + low_end, c0:]
+                a_ref[c0 + low_end:c0 + LANES, c0:] -= stacked_dot(upper[:, :LANES], upper)[low_end:]
         for d in range(b + 1, blocks):
             d0 = d * LANES
             a_ref[d0:d0 + LANES, d0:] -= dot(r_ref[c0:c0 + LANES, d0:d0 + LANES], r_ref[c0:c0 + LANES, d0:])
@@ -309,7 +338,7 @@
 def factor(gram, depth):
     vmem = pl.BlockSpec(memory_space=pltpu.VMEM)
     return pl.pallas_call(
-        factor_kernel,
+        functools.partial(factor_kernel, 4),
         out_shape=jax.ShapeDtypeStruct((depth, depth), jnp.float32),
         in_specs=[vmem],
         out_specs=vmem,

time: 104 us -> 89.3 us (0.86)
  Pallas kernels: 103 us -> 88.5 us
    pallas_call x1, Pallas kernels: 28.2 us -> 13.9 us  [factor(): pl.pallas_call(functools.partial(factor_kernel, 4), out_shape=jax.ShapeDt...]
where the time goes in v2:
time: 89.3 us; the launch traced here: 89.1 us
  Pallas kernels  88.5 us (99%)
    pallas_call x1, Pallas kernels, halo(): pl.pallas_call(functools.partial(halo_kernel, n, m), out_shape=(xs, xs, y...  42 us
    pallas_call x1, Pallas kernels, sum_over_all(): pl.pallas_call(functools.partial(sum_kernel, stages), out_shape=jax.Shape...  26.1 us
    pallas_call x1, Pallas kernels, factor(): pl.pallas_call(functools.partial(factor_kernel, 4), out_shape=jax.ShapeDt...  13.9 us
    pallas_call x1, Pallas kernels, stencil(): pl.pallas_call(functools.partial(stencil_kernel, n, m, rows, 32), out_sha...  6.53 us

profile of v2, /device:TPU:0, one launch (start us, length us, event | category | flops | bytes accessed | tf_op | source)
XLA Modules:
  0.0 89.1 jit_solution(15745282471696493502)
XLA Ops:
  0.6 42.0 %halo.1 = (f32[3,192,384]{2,1,0:T(8,128)}, f32[3,192,384]{2,1,0:T(8,128)}, f32[3,2,8,384]{3,2,1,0:T(8,128)}, f32[3,2,8,384]{3,2,1,0:T(8,128)}) custom-call(f32[2,192,384]{2,1,0:T(8,128)} %f_ref.3, f32[2,192,384]{2,1,0:T(8,128)} %o_ref.3, f32[2,192,384]{2,1,0:T(8,128)} %k_ref.3), custom_call_target="tpu_custom_call" | custom-call | tf_op jit(solution)/shard_map/halo/pallas_call | solution.py:76
  42.6 6.5 %stencil.1 = (f32[2,192,384]{2,1,0:T(8,128)}, f32[2,192,384]{2,1,0:T(8,128)}, f32[768,128]{1,0:T(8,128)}) custom-call(f32[2,192,384]{2,1,0:T(8,128)} %f_ref.3, f32[2,192,384]{2,1,0:T(8,128)} %o_ref.3, f32[2,192,384]{2,1,0:T(8,128)} %k_ref.3, f32[2,192,384]{2,1,0:T(8,128)} %r_ref.1, f32[3,192,384]{2,1,0:T(8,128)} %get-tuple-element.10.xlo, ...), custom_call_target="tpu_custom_call" | custom-call | tf_op jit(solution)/shard_map/stencil/pallas_call | solution.py:148
  49.1 26.1 %allsum.1.g_ref = f32[768,128]{1,0:T(8,128)} custom-call(f32[768,128]{1,0:T(8,128)} %get-tuple-element.16.g_ref), custom_call_target="tpu_custom_call" | custom-call | tf_op jit(solution)/shard_map/allsum/pallas_call | solution.py:241
  75.2 13.9 %factor.1 = f32[384,384]{1,0:T(8,128)} custom-call(f32[768,128]{1,0:T(8,128)} %allsum.1.g_ref), custom_call_target="tpu_custom_call" | custom-call | tf_op jit(solution)/shard_map/factor/pallas_call | solution.py:340

commit v3 on v2

v3 whole, which is shorter than its diff:
```python
import functools

import jax
import jax.numpy as jnp
from jax import lax
from jax.experimental import pallas as pl
from jax.experimental.pallas import tpu as pltpu
from jax.sharding import PartitionSpec as P

MESH = pl.DeviceIdType.MESH
TILE = 8
LANES = 128
HIGHEST = lax.Precision.HIGHEST


def peer(index, stage, k):
    axis, stride, size = stage
    mine = lax.rem(index[axis] // stride, size)
    other = lax.rem(mine + k, size)
    place = dict(index)
    place[axis] = index[axis] + (other - mine) * stride
    return mine, other, (place["gx"], place["gy"])


def sum_over_all(index, stages, source, out_ref, inbox, held, sems):
    count = len(stages)
    length = source.shape[0]
    starts = []
    start = 0
    for s, stage in enumerate(stages):
        size = stage[2]
        length //= size
        sent = []
        for k in range(1, size):
            mine, other, device = peer(index, stage, k)
            sent.append(
                pltpu.make_async_remote_copy(
                    src_ref=source.at[pl.ds(pl.multiple_of(other * length, TILE), length)],
                    dst_ref=inbox[s].at[k - 1],
                    send_sem=sems[0].at[s, k - 1],
                    recv_sem=sems[1].at[s, k - 1],
                    device_id=device,
                    device_id_type=MESH,
                )
            )
            sent[-1].start()
        for copy in sent:
            copy.wait_recv()
        total = source[pl.ds(pl.multiple_of(mine * length, TILE), length)]
        for k in range(1, size):
            total = total + inbox[s][k - 1]
        held[s][...] = total
        for copy in sent:
            copy.wait_send()
        source = held[s]
        start = start + mine * length
        starts.append((start, length))
    part = pl.ds(pl.multiple_of(start, TILE), length)
    out_ref[part] = source[...]
    for s in reversed(range(count)):
        start, length = starts[s]
        part = pl.ds(pl.multiple_of(start, TILE), length)
        sent = []
        for k in range(1, stages[s][2]):
            sent.append(
                pltpu.make_async_remote_copy(
                    src_ref=out_ref.at[part],
                    dst_ref=out_ref.at[part],
                    send_sem=sems[2].at[s, k - 1],
                    recv_sem=sems[3].at[s, k - 1],
                    device_id=peer(index, stages[s], k)[2],
                    device_id_type=MESH,
                )
            )
            sent[-1].start()
        for copy in sent:
            copy.wait()


def update_kernel(
    n, m, rows, parts, stages,
    f_hbm, o_hbm, k_hbm, r_hbm, fn_hbm, on_hbm, g_out,
    f_ref, o_ref, k_ref, r_ref, fn_ref, on_ref, xlo, xhi, ylo, yhi, gram,
    local_sem, xs_sem, xr_sem, ys_sem, yr_sem, *scratch
):
    i, j = lax.axis_index("gx"), lax.axis_index("gy")
    index = {"gx": i, "gy": j}
    planes, width, depth = f_ref.shape
    step = width // parts
    sides = (
        (i < n - 1, i > 0, i + 1, j),
        (i > 0, i < n - 1, i - 1, j),
        (j < m - 1, j > 0, i, j + 1),
        (j > 0, j < m - 1, i, j - 1),
    )
    barrier = pltpu.get_barrier_semaphore()
    greeted = sum(has.astype(jnp.int32) for has, _, _, _ in sides)
    for has, _, a, b in sides:
        @pl.when(has)
        def _(a=a, b=b):
            pl.semaphore_signal(barrier, inc=1, device_id=(a, b), device_id_type=MESH)
    for stage in stages:
        for k in range(1, stage[2]):
            pl.semaphore_signal(barrier, inc=1, device_id=peer(index, stage, k)[2], device_id_type=MESH)
            greeted = greeted + 1
    pl.semaphore_wait(barrier, greeted)
    fields = (f_hbm, o_hbm, k_hbm)

    def x_copies(side, part):
        _, _, a, b = sides[side]
        cut = pl.ds(part * step, step)
        return [
            pltpu.make_async_remote_copy(
                src_ref=ref.at[(planes - 1, 0)[side], cut],
                dst_ref=(xlo, xhi)[side].at[t, cut],
                send_sem=xs_sem.at[side, part, t],
                recv_sem=xr_sem.at[side, part, t],
                device_id=(a, b),
                device_id_type=MESH,
            )
            for t, ref in enumerate(fields)
        ]

    def y_copies(side):
        _, _, a, b = sides[2 + side]
        return [
            pltpu.make_async_remote_copy(
                src_ref=ref.at[:, pl.ds((width - TILE, 0)[side], TILE)],
                dst_ref=(ylo, yhi)[side].at[t],
                send_sem=ys_sem.at[side, t],
                recv_sem=yr_sem.at[side, t],
                device_id=(a, b),
                device_id_type=MESH,
            )
            for t, ref in enumerate(fields)
        ]

    for side in range(2):
        @pl.when(sides[2 + side][0])
        def _(side=side):
            for copy in y_copies(side):
                copy.start()
    for part in range(parts):
        for side in range(2):
            @pl.when(sides[side][0])
            def _(side=side, part=part):
                for copy in x_copies(side, part):
                    copy.start()
    loads = [
        pltpu.make_async_copy(src, dst, local_sem.at[t])
        for t, (src, dst) in enumerate(((f_hbm, f_ref), (o_hbm, o_ref), (k_hbm, k_ref), (r_hbm, r_ref)))
    ]
    for copy in loads:
        copy.start()
    for copy in loads:
        copy.wait()
    for side in range(2):
        @pl.when(sides[2 + side][1])
        def _(side=side):
            for copy in y_copies(side):
                copy.wait_recv()

    row = lax.broadcasted_iota(jnp.int32, (step, depth), 0)
    lane = lax.broadcasted_iota(jnp.int32, (step, depth), 1)
    refs = (f_ref, o_ref, k_ref)
    zero = jnp.zeros((step, depth), jnp.float32)
    zrow = jnp.zeros((1, depth), jnp.float32)
    dims = (((0,), (0,)), ((), ()))
    for q in range(parts):
        for side in range(2):
            @pl.when(sides[side][1])
            def _(side=side, q=q):
                for copy in x_copies(side, q):
                    copy.wait_recv()
        y = q * step
        part = pl.ds(y, step)
        for x in range(planes):
            center = [ref[x, part] for ref in refs]
            sets = []
            if x == 0:
                sets.append([jnp.where(i > 0, xlo[t, part], zero) for t in range(3)])
            else:
                sets.append([ref[x - 1, part] for ref in refs])
            if x == planes - 1:
                sets.append([jnp.where(i < n - 1, xhi[t, part], zero) for t in range(3)])
            else:
                sets.append([ref[x + 1, part] for ref in refs])
            if y == 0:
                before = [jnp.where(j > 0, ylo[t, x, TILE - 1:TILE], zrow) for t in range(3)]
            else:
                before = [ref[x, y - 1:y] for ref in refs]
            if y + step == width:
                after = [jnp.where(j < m - 1, yhi[t, x, 0:1], zrow) for t in range(3)]
            else:
                after = [ref[x, y + step:y + step + 1] for ref in refs]
            sets.append([jnp.where(row == 0, b, pltpu.roll(c, 1, 0)) for b, c in zip(before, center)])
            sets.append([jnp.where(row == step - 1, a, pltpu.roll(c, step - 1, 0)) for a, c in zip(after, center)])
            sets.append([jnp.where(lane == 0, 0.0, pltpu.roll(c, 1, 1)) for c in center])
            sets.append([jnp.where(lane == depth - 1, 0.0, pltpu.roll(c, depth - 1, 1)) for c in center])
            fc, oc, kc = center
            df, do = zero, zero
            for fs, os, ks in sets:
                weight = 0.5 * (kc + ks)
                df = df + weight * (fs - fc)
                do = do + weight * (os - oc)
            prod = fc * oc
            react = r_ref[x, part] * prod / jnp.sqrt(1.0 + prod * prod)
            fn_ref[x, part] = fc + 0.15 * (df - react)
            on_ref[x, part] = oc + 0.15 * (do + react)
        u = jnp.concatenate([ref[x, part] for ref in (fn_ref, on_ref) for x in range(planes)], axis=0)
        at = 0
        for a in range(0, depth, LANES):
            total = lax.dot_general(u[:, a:a + LANES], u[:, a:], dims, precision=HIGHEST, preferred_element_type=jnp.float32)
            for b in range(0, depth - a, LANES):
                block = total[:, b:b + LANES]
                held_rows = slice(at, at + LANES)
                gram[held_rows] = block if q == 0 else gram[held_rows] + block
                at += LANES
    stores = [
        pltpu.make_async_copy(src, dst, local_sem.at[t])
        for t, (src, dst) in enumerate(((fn_ref, fn_hbm), (on_ref, on_hbm)))
    ]
    for copy in stores:
        copy.start()
    gram[...] = gram[...] / rows
    if stages:
        count = len(stages)
        sum_over_all(index, stages, gram, g_out, scratch[:count], scratch[count:2 * count], scratch[2 * count:])
    else:
        g_out[...] = gram[...]
    for side in range(2):
        @pl.when(sides[2 + side][0])
        def _(side=side):
            for copy in y_copies(side):
                copy.wait_send()

        @pl.when(sides[side][0])
        def _(side=side):
            for part in range(parts):
                for copy in x_copies(side, part):
                    copy.wait_send()
    for copy in stores:
        copy.wait()


def update(n, m, rows, stages, fuel, oxidizer, kappa, rate):
    planes, width, depth = fuel.shape
    blocks = depth // LANES
    parts = 4 if width % (4 * TILE) == 0 else 1
    gram_rows = blocks * (blocks + 1) // 2 * LANES
    scratch = [pltpu.VMEM(fuel.shape, jnp.float32)] * 6
    scratch += [pltpu.VMEM((3, width, depth), jnp.float32)] * 2
    scratch += [pltpu.VMEM((3, planes, TILE, depth), jnp.float32)] * 2
    scratch += [pltpu.VMEM((gram_rows, LANES), jnp.float32)]
    scratch += [pltpu.SemaphoreType.DMA((4,))]
    scratch += [pltpu.SemaphoreType.DMA((2, parts, 3))] * 2
    scratch += [pltpu.SemaphoreType.DMA((2, 3))] * 2
    if stages:
        inbox, held, length = [], [], gram_rows
        for _, _, size in stages:
            length //= size
            inbox.append(pltpu.VMEM((size - 1, length, LANES), jnp.float32))
            held.append(pltpu.VMEM((length, LANES), jnp.float32))
        most = max(stage[2] for stage in stages)
        scratch += inbox + held + [pltpu.SemaphoreType.DMA((len(stages), most - 1))] * 4
    field = jax.ShapeDtypeStruct(fuel.shape, jnp.float32)
    any_spec = pl.BlockSpec(memory_space=pl.ANY)
    return pl.pallas_call(
        functools.partial(update_kernel, n, m, rows, parts, stages),
        out_shape=(field, field, jax.ShapeDtypeStruct((gram_rows, LANES), jnp.float32)),
        in_specs=[any_spec] * 4,
        out_specs=(any_spec, any_spec, pl.BlockSpec(memory_space=pltpu.VMEM)),
        scratch_shapes=scratch,
        compiler_params=pltpu.CompilerParams(collective_id=0, has_side_effects=True),
        name="update",
    )(fuel, oxidizer, kappa, rate)


def stacked_dot(left, right):
    dims = (((0,), (0,)), ((), ()))
    def pieces(v):
        h = v.astype(jnp.bfloat16).astype(jnp.float32)
        m = (v - h).astype(jnp.bfloat16).astype(jnp.float32)
        return h, m, v - h - m
    (a, b, c), (d, e, f) = pieces(left), pieces(right)
    lhs = jnp.concatenate([a, a, b, a, c, b], axis=0).astype(jnp.bfloat16)
    rhs = jnp.concatenate([d, e, d, f, d, e], axis=0).astype(jnp.bfloat16)
    return lax.dot_general(lhs, rhs, dims, preferred_element_type=jnp.float32)


def column_of(panel, at):
    return jnp.broadcast_to(panel[:, at:at + 1], (TILE, LANES))


def factor_kernel(group, g_ref, fn_in, on_in, r_ref, fn_out, on_out, a_ref, fn_ref, on_ref, sems):
    loads = [pltpu.make_async_copy(fn_in, fn_ref, sems.at[0]), pltpu.make_async_copy(on_in, on_ref, sems.at[1])]
    stores = [pltpu.make_async_copy(fn_ref, fn_out, sems.at[2]), pltpu.make_async_copy(on_ref, on_out, sems.at[3])]
    for copy in loads:
        copy.start()
    depth = r_ref.shape[0]
    blocks = depth // LANES
    at = 0
    for b in range(blocks):
        for c in range(b, blocks):
            a_ref[b * LANES:(b + 1) * LANES, c * LANES:(c + 1) * LANES] = g_ref[at:at + LANES]
            at += LANES
    dims = (((0,), (0,)), ((), ()))
    dot = functools.partial(lax.dot_general, dimension_numbers=dims, precision=HIGHEST, preferred_element_type=jnp.float32)
    sub = lax.broadcasted_iota(jnp.int32, (TILE, LANES), 0)
    lane = lax.broadcasted_iota(jnp.int32, (TILE, LANES), 1)
    for b in range(blocks):
        c0 = b * LANES
        tiles = range(blocks - b)
        if c0:
            r_ref[c0:c0 + LANES, :c0] = jnp.zeros((LANES, c0), jnp.float32)
        for p in range(0, LANES, TILE * group):
            before = []
            for q in range(p, p + TILE * group, TILE):
                r0 = c0 + q
                strips = [a_ref[r0:r0 + TILE, c0 + t * LANES:c0 + (t + 1) * LANES] for t in tiles]
                for s, inv, low, rows in before:
                    factors = []
                    for k in range(TILE):
                        value = column_of(strips[0], s + k)
                        for j in range(k):
                            value = value - factors[j] * low[k, j]
                        factors.append(value * inv[k])
                    for t in tiles:
                        for k in range(TILE):
                            strips[t] = strips[t] - factors[k] * rows[t][k]
                e = {}
                for k in range(TILE):
                    column = column_of(strips[0], q + k)
                    for i in range(k, TILE):
                        e[i, k] = jnp.broadcast_to(column[i:i + 1], (TILE, LANES))
                inv, low = [], {}
                for k in range(TILE):
                    inv.append(lax.rsqrt(e[k, k]))
                    for i in range(k + 1, TILE):
                        low[i, k] = e[i, k] * inv[k]
                    for j in range(k + 1, TILE):
                        for i in range(j, TILE):
                            e[i, j] = e[i, j] - low[i, k] * low[j, k]
                rows = []
                for t in tiles:
                    made = []
                    for k in range(TILE):
                        value = jnp.broadcast_to(strips[t][k:k + 1], (TILE, LANES))
                        for j in range(k):
                            value = value - low[k, j] * made[j]
                        made.append(value * inv[k])
                    rows.append(made)
                    strip = made[0]
                    for k in range(1, TILE):
                        strip = jnp.where(sub == k, made[k], strip)
                    if t == 0:
                        strip = jnp.where(lane >= sub + q, strip, 0.0)
                    r_ref[r0:r0 + TILE, c0 + t * LANES:c0 + (t + 1) * LANES] = strip
                before.append((q, inv, low, rows))
            low_end = p + TILE * group
            if low_end < LANES:
                upper = r_ref[c0 + p:c0 + low_end, c0:]
                a_ref[c0 + low_end:c0 + LANES, c0:] -= stacked_dot(upper[:, :LANES], upper)[low_end:]
        if b == 0:
            for load, store in zip(loads, stores):
                load.wait()
                store.start()
        for d in range(b + 1, blocks):
            d0 = d * LANES
            a_ref[d0:d0 + LANES, d0:] -= dot(r_ref[c0:c0 + LANES, d0:d0 + LANES], r_ref[c0:c0 + LANES, d0:])
    for copy in stores:
        copy.wait()


def factor(gram, fuel_next, oxid_next):
    depth = fuel_next.shape[2]
    field = jax.ShapeDtypeStruct(fuel_next.shape, jnp.float32)
    vmem = pl.BlockSpec(memory_space=pltpu.VMEM)
    any_spec = pl.BlockSpec(memory_space=pl.ANY)
    return pl.pallas_call(
        functools.partial(factor_kernel, 4),
        out_shape=(jax.ShapeDtypeStruct((depth, depth), jnp.float32), field, field),
        in_specs=[vmem, any_spec, any_spec],
        out_specs=(vmem, any_spec, any_spec),
        scratch_shapes=[
            pltpu.VMEM((depth, depth), jnp.float32),
            pltpu.VMEM(fuel_next.shape, jnp.float32),
            pltpu.VMEM(fuel_next.shape, jnp.float32),
            pltpu.SemaphoreType.DMA((4,)),
        ],
        name="factor",
    )(gram, fuel_next, oxid_next)


def shards(n, m, fuel, oxidizer, kappa, rate):
    planes, width, depth = fuel.shape
    rows = 2 * planes * width * n * m
    blocks = depth // LANES
    stages = ()
    if blocks * (blocks + 1) // 2 * LANES % (TILE * n * m) == 0:
        pairs = [("gy", 1, 2), ("gy", 2, 2)] if m == 4 else [("gy", 1, m)]
        stages = tuple(pairs + [("gx", 1, n)])
    fuel_next, oxid_next, gram = update(n, m, rows, stages, fuel, oxidizer, kappa, rate)
    if not stages:
        gram = lax.psum(gram, ("gx", "gy"))
    r_factor, fuel_next, oxid_next = factor(gram, fuel_next, oxid_next)
    return (fuel_next, oxid_next, r_factor)


def solution(mesh):
    spec = P("gx", "gy", None)
    body = functools.partial(shards, mesh.shape["gx"], mesh.shape["gy"])
    return jax.shard_map(body, mesh=mesh, in_specs=(spec,) * 4, out_specs=(spec, spec, P()), check_vma=False)
```

time: 89.3 us -> 83.5 us (0.935)
  Pallas kernels: 88.5 us -> 82.6 us
    pallas_call x4 -> x2, Pallas kernels: 88.5 us -> 82.6 us  [the longest x1 67.5 us: update(): pl.pallas_call(functools.partial(update_kernel, n, m, rows, parts, stages...]
where the time goes in v3:
time: 83.5 us; the launch traced here: 83.3 us
  Pallas kernels  82.6 us (99%)
    pallas_call x1, Pallas kernels, update(): pl.pallas_call(functools.partial(update_kernel, n, m, rows, parts, stages...  67.5 us
    pallas_call x1, Pallas kernels, factor(): pl.pallas_call(functools.partial(factor_kernel, 4), out_shape=(jax.ShapeD...  15.1 us

profile of v3, /device:TPU:0, one launch (start us, length us, event | category | flops | bytes accessed | tf_op | source)
XLA Modules:
  0.0 83.3 jit_solution(5612001093990308008)
XLA Ops:
  0.6 67.5 %update.1 = (f32[2,192,384]{2,1,0:T(8,128)}, f32[2,192,384]{2,1,0:T(8,128)}, f32[768,128]{1,0:T(8,128)}) custom-call(f32[2,192,384]{2,1,0:T(8,128)} %f_hbm.1, f32[2,192,384]{2,1,0:T(8,128)} %o_hbm.1, f32[2,192,384]{2,1,0:T(8,128)} %k_hbm.1, f32[2,192,384]{2,1,0:T(8,128)} %r_hbm.1), custom_call_target="tpu_custom_call" | custom-call | tf_op jit(solution)/shard_map/update/pallas_call | solution.py:268
  68.1 15.1 %factor.1 = (f32[384,384]{1,0:T(8,128)}, f32[2,192,384]{2,1,0:T(8,128)}, f32[2,192,384]{2,1,0:T(8,128)}) custom-call(f32[768,128]{1,0:T(8,128)} %get-tuple-element.9.g_ref, f32[2,192,384]{2,1,0:T(8,128)} %get-tuple-element.10.fn_in, f32[2,192,384]{2,1,0:T(8,128)} %get-tuple-element.11.on_in), custom_call_target="tpu_custom_call" | custom-call | tf_op jit(solution)/shard_map/factor/pallas_call | solution.py:380

commit v4 on v3

--- a/solution.py
+++ b/solution.py
@@ -80,8 +80,8 @@
 def update_kernel(
     n, m, rows, parts, stages,
     f_hbm, o_hbm, k_hbm, r_hbm, fn_hbm, on_hbm, g_out,
-    f_ref, o_ref, k_ref, r_ref, fn_ref, on_ref, xlo, xhi, ylo, yhi, gram,
-    local_sem, xs_sem, xr_sem, ys_sem, yr_sem, *scratch
+    f_ref, o_ref, k_ref, r_ref, fn_ref, on_ref, xlo, xhi, ylo, yhi, gram, passing,
+    local_sem, xs_sem, xr_sem, ys_sem, yr_sem, ps_sem, pr_sem, *scratch
 ):
     i, j = lax.axis_index("gx"), lax.axis_index("gy")
     index = {"gx": i, "gy": j}
@@ -93,9 +93,23 @@
         (j < m - 1, j > 0, i, j + 1),
         (j > 0, j < m - 1, i, j - 1),
     )
+    z, odd, depth_z = i // 2, lax.rem(i, 2) == 1, n // 2
+    rising = lambda pair: (pair + 1) * parts // depth_z
+    falling = lambda pair: (depth_z - 1 - pair) * parts // depth_z
+    if n % 2 or n < 4:
+        indirect = (0, 0)
+        relayed = 0
+    else:
+        indirect = (jnp.where(odd, falling(z), 0), jnp.where(odd, 0, rising(z - 1)))
+        relayed = jnp.where(odd, rising(z - 1), falling(z))
+    via = (i - 1, i + 1)
+    onward = jnp.where(odd, i - 2, i + 2)
+    lands = (jnp.logical_not(odd), odd)
+    relayed = jnp.where(odd, jnp.where(z > 0, relayed, 0), jnp.where(z < depth_z - 1, relayed, 0))
+    greets = sides + ((i < n - 2, None, i + 2, j), (i > 1, None, i - 2, j))
     barrier = pltpu.get_barrier_semaphore()
-    greeted = sum(has.astype(jnp.int32) for has, _, _, _ in sides)
-    for has, _, a, b in sides:
+    greeted = sum(has.astype(jnp.int32) for has, _, _, _ in greets)
+    for has, _, a, b in greets:
         @pl.when(has)
         def _(a=a, b=b):
             pl.semaphore_signal(barrier, inc=1, device_id=(a, b), device_id_type=MESH)
@@ -121,6 +135,34 @@
             for t, ref in enumerate(fields)
         ]
 
+    def to_relay(side, part):
+        cut = pl.ds(part * step, step)
+        return [
+            pltpu.make_async_remote_copy(
+                src_ref=ref.at[(planes - 1, 0)[side], cut],
+                dst_ref=passing.at[t, cut],
+                send_sem=xs_sem.at[side, part, t],
+                recv_sem=pr_sem.at[part, t],
+                device_id=(via[side], j),
+                device_id_type=MESH,
+            )
+            for t, ref in enumerate(fields)
+        ]
+
+    def from_relay(side, part):
+        cut = pl.ds(part * step, step)
+        return [
+            pltpu.make_async_remote_copy(
+                src_ref=passing.at[t, cut],
+                dst_ref=(xlo, xhi)[side].at[t, cut],
+                send_sem=ps_sem.at[part, t],
+                recv_sem=xr_sem.at[side, part, t],
+                device_id=(onward, j),
+                device_id_type=MESH,
+            )
+            for t in range(3)
+        ]
+
     def y_copies(side):
         _, _, a, b = sides[2 + side]
         return [
@@ -142,9 +184,14 @@
                 copy.start()
     for part in range(parts):
         for side in range(2):
-            @pl.when(sides[side][0])
+            @pl.when(sides[side][0] & (part >= indirect[side]))
             def _(side=side, part=part):
                 for copy in x_copies(side, part):
+                    copy.start()
+
+            @pl.when(sides[side][0] & (part < indirect[side]))
+            def _(side=side, part=part):
+                for copy in to_relay(side, part):
                     copy.start()
     loads = [
         pltpu.make_async_copy(src, dst, local_sem.at[t])
@@ -167,6 +214,17 @@
     zrow = jnp.zeros((1, depth), jnp.float32)
     dims = (((0,), (0,)), ((), ()))
     for q in range(parts):
+        @pl.when(q < relayed)
+        def _(q=q):
+            for copy in to_relay(0, q):
+                copy.wait_recv()
+
+        for side in range(2):
+            @pl.when((q < relayed) & lands[side])
+            def _(side=side, q=q):
+                for copy in from_relay(side, q):
+                    copy.start()
+
         for side in range(2):
             @pl.when(sides[side][1])
             def _(side=side, q=q):
@@ -239,6 +297,12 @@
             for part in range(parts):
                 for copy in x_copies(side, part):
                     copy.wait_send()
+
+    for part in range(parts):
+        @pl.when(part < relayed)
+        def _(part=part):
+            for copy in from_relay(0, part):
+                copy.wait_send()
     for copy in stores:
         copy.wait()
 
@@ -252,9 +316,11 @@
     scratch += [pltpu.VMEM((3, width, depth), jnp.float32)] * 2
     scratch += [pltpu.VMEM((3, planes, TILE, depth), jnp.float32)] * 2
     scratch += [pltpu.VMEM((gram_rows, LANES), jnp.float32)]
+    scratch += [pltpu.VMEM((3, width, depth), jnp.float32)]
     scratch += [pltpu.SemaphoreType.DMA((4,))]
     scratch += [pltpu.SemaphoreType.DMA((2, parts, 3))] * 2
     scratch += [pltpu.SemaphoreType.DMA((2, 3))] * 2
+    scratch += [pltpu.SemaphoreType.DMA((parts, 3))] * 2
     if stages:
         inbox, held, length = [], [], gram_rows
         for _, _, size in stages:

time: 83.5 us -> 79.1 us (0.947)
  Pallas kernels: 82.6 us -> 78.2 us
    pallas_call x1, Pallas kernels: 67.5 us -> 63.1 us  [update(): pl.pallas_call(functools.partial(update_kernel, n, m, rows, parts, stages...]
where the time goes in v4:
time: 79.1 us; the launch traced here: 78.9 us
  Pallas kernels  78.2 us (99%)
    pallas_call x1, Pallas kernels, update(): pl.pallas_call(functools.partial(update_kernel, n, m, rows, parts, stages...  63.1 us
    pallas_call x1, Pallas kernels, factor(): pl.pallas_call(functools.partial(factor_kernel, 4), out_shape=(jax.ShapeD...  15.1 us

profile of v4, /device:TPU:0, one launch (start us, length us, event | category | flops | bytes accessed | tf_op | source)
XLA Modules:
  0.0 78.9 jit_solution(18381226980398563536)
XLA Ops:
  0.6 63.1 %update.1 = (f32[2,192,384]{2,1,0:T(8,128)}, f32[2,192,384]{2,1,0:T(8,128)}, f32[768,128]{1,0:T(8,128)}) custom-call(f32[2,192,384]{2,1,0:T(8,128)} %f_hbm.1, f32[2,192,384]{2,1,0:T(8,128)} %o_hbm.1, f32[2,192,384]{2,1,0:T(8,128)} %k_hbm.1, f32[2,192,384]{2,1,0:T(8,128)} %r_hbm.1), custom_call_target="tpu_custom_call" | custom-call | tf_op jit(solution)/shard_map/update/pallas_call | solution.py:334
  63.8 15.1 %factor.1 = (f32[384,384]{1,0:T(8,128)}, f32[2,192,384]{2,1,0:T(8,128)}, f32[2,192,384]{2,1,0:T(8,128)}) custom-call(f32[768,128]{1,0:T(8,128)} %get-tuple-element.9.g_ref, f32[2,192,384]{2,1,0:T(8,128)} %get-tuple-element.10.fn_in, f32[2,192,384]{2,1,0:T(8,128)} %get-tuple-element.11.on_in), custom_call_target="tpu_custom_call" | custom-call | tf_op jit(solution)/shard_map/factor/pallas_call | solution.py:446

commit v5 on v4

--- a/solution.py
+++ b/solution.py
@@ -310,7 +310,7 @@
 def update(n, m, rows, stages, fuel, oxidizer, kappa, rate):
     planes, width, depth = fuel.shape
     blocks = depth // LANES
-    parts = 4 if width % (4 * TILE) == 0 else 1
+    parts = 8 if width % (8 * TILE) == 0 else 1
     gram_rows = blocks * (blocks + 1) // 2 * LANES
     scratch = [pltpu.VMEM(fuel.shape, jnp.float32)] * 6
     scratch += [pltpu.VMEM((3, width, depth), jnp.float32)] * 2

time: 79.1 us -> 79.1 us (level)
  no operation moved by 1% of the time
where the time goes in v5:
time: 79.1 us; the launch traced here: 78.9 us
  Pallas kernels  78.3 us (99%)
    pallas_call x1, Pallas kernels, update(): pl.pallas_call(functools.partial(update_kernel, n, m, rows, parts, stages...  63.2 us
    pallas_call x1, Pallas kernels, factor(): pl.pallas_call(functools.partial(factor_kernel, 4), out_shape=(jax.ShapeD...  15.1 us

profile of v5, /device:TPU:0, one launch (start us, length us, event | category | flops | bytes accessed | tf_op | source)
XLA Modules:
  0.0 78.9 jit_solution(8706770392055886650)
XLA Ops:
  0.6 63.2 %update.1 = (f32[2,192,384]{2,1,0:T(8,128)}, f32[2,192,384]{2,1,0:T(8,128)}, f32[768,128]{1,0:T(8,128)}) custom-call(f32[2,192,384]{2,1,0:T(8,128)} %f_hbm.1, f32[2,192,384]{2,1,0:T(8,128)} %o_hbm.1, f32[2,192,384]{2,1,0:T(8,128)} %k_hbm.1, f32[2,192,384]{2,1,0:T(8,128)} %r_hbm.1), custom_call_target="tpu_custom_call" | custom-call | tf_op jit(solution)/shard_map/update/pallas_call | solution.py:334
  63.8 15.1 %factor.1 = (f32[384,384]{1,0:T(8,128)}, f32[2,192,384]{2,1,0:T(8,128)}, f32[2,192,384]{2,1,0:T(8,128)}) custom-call(f32[768,128]{1,0:T(8,128)} %get-tuple-element.9.g_ref, f32[2,192,384]{2,1,0:T(8,128)} %get-tuple-element.10.fn_in, f32[2,192,384]{2,1,0:T(8,128)} %get-tuple-element.11.on_in), custom_call_target="tpu_custom_call" | custom-call | tf_op jit(solution)/shard_map/factor/pallas_call | solution.py:446
